TPU v7x, 32 devices: a whole 2x2x4 slice. The times are simulated.
32 devices in a mesh: req: 8 (over z, x), tp: 4 (over y, core).
Axes of the slice: x: 2, y: 2, z: 4, core: 2. Of those that a mesh axis runs over, the one named last changes fastest.
Arguments:
- hidden_in: bfloat16 [8, 1024, 2048], P('req', None, 'tp'), may hold values from -6 to 6
- ln_gain: float32 [2048], replicated, may hold values from 0.25 to 1.75
- ln_bias: float32 [2048], replicated, may hold values from -1.5 to 1.5
- w_qkv: bfloat16 [3, 2048, 2048], P(None, None, 'tp'), may hold values from -0.125 to 0.125
- b_qkv: float32 [3, 2048], P(None, 'tp'), may hold values from -1.5 to 1.5
- w_out: bfloat16 [2048, 2048], P('tp'), may hold values from -0.125 to 0.125
- b_out: float32 [2048], replicated, may hold values from -1.5 to 1.5
- alibi_slope: float32 [16], P('tp'), may hold values from 2.4414063e-05 to 0.1
- prefix_k: bfloat16 [2048, 2048], P('req', 'tp'), may hold values from -160 to 160
- prefix_v: bfloat16 [2048, 2048], P('req', 'tp'), may hold values from -6 to 6
- suffix_len: int32 [8], P('req'), may hold values from 64 to 1024, as said below
- group_of: int32 [8], P('req'), may hold values from 0 to 1
- block_of_device: int32 [8], P('req'), may hold values from 0 to 7, each once
Outputs:
- mixed: bfloat16 [8, 1024, 2048], P('req', None, 'tp')
- cache_k: bfloat16 [8, 1024, 2048], P('req', None, 'tp')
- cache_v: bfloat16 [8, 1024, 2048], P('req', None, 'tp')
Inputs may be any that keep to these rules, and one draw needn't show every extreme that they name: `suffix_len`: every request has at least 64 live slots; some request has exactly 1024.
All inputs are finite; a program needn't handle non-finite values.
Results may differ from a plain program's by a relative error of at most 0.011.
Values may be sent and summed in bfloat16 or wider, within the bound.
A program may use at most 384 MiB of HBM per device.

v0:
```python
import jax
import jax.numpy as jnp
from jax import lax
from jax.sharding import PartitionSpec as P

EPS = 1e-05
NEGATIVE = -1e30


def on_device(
    hidden_in,
    ln_gain,
    ln_bias,
    w_qkv,
    b_qkv,
    w_out,
    b_out,
    alibi_slope,
    prefix_k,
    prefix_v,
    suffix_len,
    group_of,
    block_of_device,
):
    local_rows = hidden_in[0]
    slots = local_rows.shape[0]
    width_dev = local_rows.shape[1]
    gathered = lax.all_gather(local_rows, "tp", axis=1, tiled=True)
    values32 = gathered.astype(jnp.float32)
    center = values32 - jnp.mean(values32, axis=1, keepdims=True)
    spread = jnp.mean(center * center, axis=1, keepdims=True)
    normed = (center / jnp.sqrt(spread + EPS) * ln_gain + ln_bias).astype(jnp.bfloat16)
    projected = (
        jnp.einsum("sd,cdh->csh", normed, w_qkv, preferred_element_type=jnp.float32)
        + b_qkv[:, None, :]
    )
    projected = projected.astype(jnp.bfloat16)
    query, keys, values = (projected[0], projected[1], projected[2])
    length = suffix_len[0]
    my_group = group_of[0]
    slot_ids = lax.iota(jnp.int32, slots)
    live = slot_ids < length
    keys_out = jnp.where(live[:, None], keys, jnp.zeros_like(keys))
    values_out = jnp.where(live[:, None], values, jnp.zeros_like(values))
    heads_dev = alibi_slope.shape[0]
    head_size = query.shape[1] // heads_dev
    attn_scale = 1.0 / jnp.sqrt(jnp.float32(head_size))
    query_heads = query.reshape(slots, heads_dev, head_size)
    block_tokens = prefix_k.shape[0]
    half_count = lax.axis_size("req") // 2
    prefix_total = half_count * block_tokens
    block_numbers = jnp.full((block_tokens,), block_of_device[0], jnp.int32)
    query_pos = (prefix_total + slot_ids).astype(jnp.float32)
    key_piece = lax.all_gather(prefix_k, "req", axis=0, tiled=True)
    value_piece = lax.all_gather(prefix_v, "req", axis=0, tiled=True)
    number_piece = lax.all_gather(block_numbers, "req", axis=0, tiled=True)
    count = key_piece.shape[0]
    offsets = lax.iota(jnp.int32, count) % block_tokens
    key_pos = (number_piece % half_count * block_tokens + offsets).astype(jnp.float32)
    fold_allowed = number_piece // half_count == my_group
    compute_old_max = jnp.full((heads_dev, slots), NEGATIVE, jnp.float32)
    compute_key_heads = key_piece.reshape(count, heads_dev, head_size)
    compute_value_heads = value_piece.reshape(count, heads_dev, head_size)
    compute_scores = (
        jnp.einsum(
            "shd,khd->hsk", query_heads, compute_key_heads, preferred_element_type=jnp.float32
        )
        * attn_scale
    )
    compute_scores = compute_scores - alibi_slope[:, None, None] * (
        query_pos[None, :, None] - key_pos[None, None, :]
    )
    compute_scores = jnp.where(fold_allowed[None, None, :], compute_scores, NEGATIVE)
    compute_new_max = jnp.maximum(compute_old_max, jnp.max(compute_scores, axis=2))
    compute_weights = jnp.where(
        fold_allowed[None, None, :], jnp.exp(compute_scores - compute_new_max[:, :, None]), 0.0
    )
    compute_new_sum = jnp.sum(compute_weights, axis=2)
    compute_new_acc = jnp.einsum(
        "hsk,khd->hsd",
        compute_weights.astype(jnp.bfloat16),
        compute_value_heads,
        preferred_element_type=jnp.float32,
    )
    key_heads = keys.reshape(slots, heads_dev, head_size)
    value_heads = values.reshape(slots, heads_dev, head_size)
    row_block = min(512, slots)
    pieces_out = []
    for row_start in range(0, slots, row_block):
        row_stop = min(slots, row_start + row_block)
        row_ids = slot_ids[row_start:row_stop]
        query_block = query_heads[row_start:row_stop]
        scores = (
            jnp.einsum("shd,khd->hsk", query_block, key_heads, preferred_element_type=jnp.float32)
            * attn_scale
        )
        scores = (
            scores
            - alibi_slope[:, None, None]
            * (row_ids[:, None] - slot_ids[None, :]).astype(jnp.float32)[None]
        )
        allowed = (slot_ids[None, :] <= row_ids[:, None]) & (slot_ids[None, :] < length)
        scores = jnp.where(allowed[None], scores, NEGATIVE)
        old_max = compute_new_max[:, row_start:row_stop]
        new_max = jnp.maximum(old_max, jnp.max(scores, axis=2))
        weights = jnp.where(allowed[None], jnp.exp(scores - new_max[:, :, None]), 0.0)
        factor = jnp.exp(old_max - new_max)
        new_sum = compute_new_sum[:, row_start:row_stop] * factor + jnp.sum(weights, axis=2)
        new_acc = compute_new_acc[:, row_start:row_stop] * factor[:, :, None] + jnp.einsum(
            "hsk,khd->hsd",
            weights.astype(jnp.bfloat16),
            value_heads,
            preferred_element_type=jnp.float32,
        )
        piece_out = new_acc / new_sum[:, :, None]
        pieces_out.append(piece_out)
    attended = jnp.concatenate(pieces_out, axis=1)
    attended = (
        attended.transpose(1, 0, 2).reshape(slots, heads_dev * head_size).astype(jnp.bfloat16)
    )
    partial_value = jnp.dot(attended, w_out, preferred_element_type=jnp.float32)
    summed = lax.psum_scatter(
        partial_value.astype(jnp.bfloat16), "tp", scatter_dimension=1, tiled=True
    ).astype(jnp.float32)
    bias_part = lax.dynamic_slice_in_dim(b_out, lax.axis_index("tp") * width_dev, width_dev)
    result = summed + bias_part + local_rows.astype(jnp.float32)
    result = jnp.where(live[:, None], result, 0.0).astype(jnp.bfloat16)
    return (result[None], keys_out[None], values_out[None])


def solution(mesh):
    return jax.shard_map(
        on_device,
        mesh=mesh,
        in_specs=(
            P("req", None, "tp"),
            P(),
            P(),
            P(None, None, "tp"),
            P(None, "tp"),
            P("tp", None),
            P(),
            P("tp"),
            P("req", "tp"),
            P("req", "tp"),
            P("req"),
            P("req"),
            P("req"),
        ),
        out_specs=(P("req", None, "tp"), P("req", None, "tp"), P("req", None, "tp")),
        check_vma=False,
    )
```

profile of v0, /device:TPU:0, one launch (start us, length us, event | category | flops | bytes accessed | tf_op | source)
XLA Modules:
  0.0 241.2 jit_solution(5262396388451075236)
XLA Ops:
  7.2 0.0 copy-start
  7.2 0.0 all-gather.10.cloned.1.call-start
  7.2 0.7 all-gather.10.cloned.1.call-update
  7.9 0.0 all-gather.6.cloned.1.call-start
  8.0 1.8 copy.42
  9.8 0.0 all-gather.6.cloned.1.call-update
  9.8 0.0 all-gather.8.cloned.1.call-start
  9.8 1.8 copy.45
  11.6 0.0 all-gather.8.cloned.1.call-update
  11.6 0.0 reduce-scatter.2.cloned.1.call-start
  12.4 2.4 subtract_convert_fusion
  14.8 1.8 fusion.35
  17.2 22.2 %all-gather.1 = s32[8,1,256]{2,1,0:T(1,128)S(1)} all-gather(s32[1,1,256]{2,1,0:T(1,128)S(1)} %broadcast.168), channel_id=1, replica_groups=mesh['req'=8,'tp'=4] {'req'}, dimensions={0}, use_global_device_ids=true | all-gather | bytes 9216 | tf_op jit(solution)/shard_map/all_gather | solution.py:56
  40.2 0.0 copy-start.15
  40.2 0.0 copy-start.16
  40.2 0.0 copy-start.17
  40.2 3.8 %broadcast_subtract_fusion = f32[1024,2048]{1,0:T(8,128)} fusion(f32[2048]{0:T(1024)S(1)} %fusion.50, f32[1024]{0:T(1024)S(1)} %add_convert_fusion.1), kind=kLoop, calls=%fused_computation.28 | loop fusion | flops 2097152 | bytes 8400896 | tf_op jit(solution)/shard_map/sub | solution.py:71
  44.0 2.8 %all-gather.10.cloned.1.call-done = bf16[1,1024,2048]{2,1,0:T(8,128)(2,1)} async-done(((bf16[1,1024,512]{2,1,0:T(8,128)(2,1)}), bf16[1,1024,2048]{2,1,0:T(8,128)(2,1)}) %all-gather.10.cloned.1.call-update) | async-done | bytes 4194320 | tf_op jit(solution)/shard_map/all_gather | solution.py:28
  46.8 3.0 %convert_reduce_fusion = f32[1024]{0:T(1024)S(1)} fusion(bf16[1,1024,2048]{2,1,0:T(8,128)(2,1)} %all-gather.10.cloned.1.call-done), kind=kLoop, calls=%fused_computation.6 | loop fusion | flops 4193280 | bytes 4198400 | tf_op jit(solution)/shard_map/reduce_sum | solution.py:30
  49.8 3.4 %fusion.8 = f32[1024]{0:T(1024)S(1)} fusion(bf16[1,1024,2048]{2,1,0:T(8,128)(2,1)} %all-gather.10.cloned.1.call-done, f32[1024]{0:T(1024)S(1)} %broadcast_multiply_fusion), kind=kLoop, calls=%fused_computation.11 | loop fusion | flops 8387584 | bytes 4202496 | tf_op jit(solution)/shard_map/reduce_sum | solution.py:31
  53.2 0.0 copy-done.15
  53.2 0.0 copy-done.16
  53.2 0.0 copy-done.17
  53.2 11.3 %fusion.29 = bf16[3,1024,512]{1,2,0:T(8,128)(2,1)S(1)} fusion(f32[3,512]{1,0:T(4,128)S(1)} %copy-done.15, bf16[3,2048,512]{2,1,0:T(8,128)(2,1)} %param.16, bf16[1,1024,2048]{2,1,0:T(8,128)(2,1)S(1)} %copy-done.1, f32[2048]{0:T(1024)S(1)} %copy-done.16, f32[2048]{0:T(1024)S(1)} %copy-done.17, f32[1024]{0:T(1024)S(1)} %add_sqrt_fusion, ...), kind=kOutput, calls=%fused_computation.36 | convolution fusion | flops 6458179584 | bytes 13662208 | tf_op jit(solution)/shard_map/sd,cdh->csh/dot_general | solution.py:34
  64.5 0.0 copy-start.14
  64.5 2.1 broadcast_select_fusion
  66.7 1.1 fusion.65
  67.7 32.2 %all-gather.6.cloned.1.call-done = bf16[2048,512]{0,1:T(8,128)(2,1)} async-done(((bf16[256,512]{0,1:T(8,128)(2,1)}), bf16[2048,512]{0,1:T(8,128)(2,1)}) %all-gather.6.cloned.1.call-update) | async-done | bytes 2097168 | tf_op jit(solution)/shard_map/all_gather | solution.py:54
  99.9 17.8 %fusion.66 = (f32[4,1024]{1,0:T(4,128)S(1)}, f32[4,1024,2048]{2,1,0:T(8,128)}) fusion(f32[1024,2048]{1,0:T(8,128)} %broadcast_subtract_fusion, f32[4]{0:T(128)S(1)} %copy-done.14, bf16[1024,4,128]{0,2,1:T(8,128)(2,1)S(1)} %bitcast.62, bf16[2048,4,128]{0,2,1:T(8,128)(2,1)} %bitcast.63, pred[2048]{0:T(1024)(128)(4,1)S(1)} %fusion.47), kind=kOutput, calls=%fused_computation.94 | convolution fusion | flops 2189422592 | bytes 45107216 | tf_op jit(solution)/shard_map/shd,khd->hsk/dot_general | solution.py:65
  117.8 4.5 %fusion.16 = (f32[4,512]{1,0:T(4,128)S(1)}, f32[4,512,1024]{2,1,0:T(8,128)S(1)}) fusion(f32[512,1024]{1,0:T(8,128)} %get-tuple-element.35, f32[4]{0:T(128)S(1)} %copy-done.14, pred[512,1024]{1,0:T(8,128)(4,1)} %get-tuple-element.28, bf16[512,4,128]{0,2,1:T(8,128)(2,1)} %bitcast.70, bf16[1024,4,128]{0,2,1:T(8,128)(2,1)} %bitcast.66), kind=kOutput, calls=%fused_computation.24 | convolution fusion | flops 547354624 | bytes 12591120 | tf_op jit(solution)/shard_map/shd,khd->hsk/dot_general | solution.py:94
  122.4 7.8 %fusion.12 = (f32[4,512]{1,0:T(4,128)S(1)}, f32[4,512]{1,0:T(4,128)S(1)}, f32[4,512,1024]{2,1,0:T(8,128)}) fusion(f32[4,512,1024]{2,1,0:T(8,128)S(1)} %get-tuple-element.30, f32[4,512]{1,0:T(4,128)S(1)} %slice_maximum_fusion.1, f32[512,1024]{1,0:T(8,128)S(1)} %copy-done.7, f32[4]{0:T(128)S(1)} %copy-done.14, pred[512,1024]{1,0:T(8,128)(4,1)S(1)} %copy-done.11, ...), kind=kOutput, calls=%fused_computation.19 | convolution fusion | flops 562032640 | bytes 23617552 | tf_op jit(solution)/shard_map/shd,khd->hsk/dot_general | solution.py:94
  130.2 14.3 %fusion = f32[4,1024]{1,0:T(4,128)S(1)} fusion(f32[4,1024,2048]{2,1,0:T(8,128)} %get-tuple-element.32, f32[4,1024]{1,0:T(4,128)S(1)} %broadcast_maximum_fusion, pred[2048]{0:T(1024)(128)(4,1)S(1)} %fusion.47), kind=kLoop, calls=%fused_computation.2 | loop fusion | flops 25161728 | bytes 33589248 | tf_op jit(solution)/shard_map/reduce_sum | solution.py:78
  144.6 6.7 %all-gather.8.cloned.1.call-done = bf16[2048,512]{0,1:T(8,128)(2,1)} async-done(((bf16[256,512]{0,1:T(8,128)(2,1)}), bf16[2048,512]{0,1:T(8,128)(2,1)}) %all-gather.8.cloned.1.call-update) | async-done | bytes 2097168 | tf_op jit(solution)/shard_map/all_gather | solution.py:55
  151.3 15.1 %fusion.2 = f32[4,1024,128]{2,1,0:T(8,128)} fusion(bf16[2048,4,128]{0,2,1:T(8,128)(2,1)} %bitcast.73, f32[4,1024,2048]{2,1,0:T(8,128)} %get-tuple-element.32, f32[4,1024]{1,0:T(4,128)S(1)} %broadcast_maximum_fusion, pred[2048]{0:T(1024)(128)(4,1)S(1)} %fusion.47), kind=kOutput, calls=%fused_computation.4 | convolution fusion | flops 2172649472 | bytes 37767168 | tf_op jit(solution)/shard_map/hsk,khd->hsd/dot_general | solution.py:79
  166.4 0.0 slice-start
  166.4 6.0 %fusion.14 = f32[4,512]{1,0:T(4,128)S(1)} fusion(f32[4,512,1024]{2,1,0:T(8,128)} %get-tuple-element.33, f32[4,512]{1,0:T(4,128)S(1)} %slice_maximum_fusion, f32[512,1024]{1,0:T(8,128)S(1)} %copy-done.4, f32[4]{0:T(128)S(1)} %copy-done.14, pred[512,1024]{1,0:T(8,128)(4,1)S(1)} %copy-done.6), kind=kLoop, calls=%fused_computation.21 | loop fusion | flops 14678016 | bytes 11026448 | tf_op jit(solution)/shard_map/reduce_sum | solution.py:108
  172.5 0.0 slice-start.1
  172.5 5.8 %divide_convert_fusion = bf16[4,512,128]{2,1,0:T(8,128)(2,1)S(1)} fusion(bf16[1024,4,128]{0,2,1:T(8,128)(2,1)S(1)} %bitcast.64, f32[4,512,1024]{2,1,0:T(8,128)S(1)} %copy-done.2, f32[4,512]{1,0:T(4,128)S(1)} %slice_maximum_fusion, f32[512,1024]{1,0:T(8,128)S(1)} %copy-done.4, f32[4]{0:T(128)S(1)} %copy-done.14, pred[512,1024]{1,0:T(8,128)(4,1)S(1)} %copy-done.6, ...), kind=kOutput, calls=%fused_computation.52 | convolution fusion | flops 552599552 | bytes 13656080 | tf_op jit(solution)/shard_map/hsk,khd->hsd/dot_general | solution.py:109
  178.4 3.8 %divide_convert_fusion.1 = bf16[4,512,128]{2,1,0:T(8,128)(2,1)S(1)} fusion(bf16[1024,4,128]{0,2,1:T(8,128)(2,1)S(1)} %bitcast.65, f32[4,512,1024]{2,1,0:T(8,128)S(1)} %bitcast.75, f32[4,512]{1,0:T(4,128)S(1)} %slice_maximum_fusion.1, f32[512,1024]{1,0:T(8,128)S(1)} %copy-done.8, f32[4]{0:T(128)S(1)} %copy-done.14, pred[512,1024]{1,0:T(8,128)(4,1)S(1)} %copy-done.12, ...), kind=kOutput, calls=%fused_computation.53 | convolution fusion | flops 552599552 | bytes 13656080 | tf_op jit(solution)/shard_map/hsk,khd->hsd/dot_general | solution.py:109
  182.1 0.1 maximum_bitcast_fusion
  182.2 1.3 copy.53
  183.5 5.7 %convolution_convert_fusion = bf16[1024,2048]{1,0:T(8,128)(2,1)} fusion(bf16[1024,512]{0,1:T(8,128)(2,1)} %bitcast.68, bf16[512,2048]{1,0:T(8,128)(2,1)S(1)} %copy-done), kind=kOutput, calls=%fused_computation.35 | convolution fusion | flops 2149580800 | bytes 7340032 | tf_op jit(solution)/shard_map/dot_general | solution.py:121
  189.2 0.0 reduce-scatter.2.cloned.1.call-update
  189.2 0.8 dynamic_slice.3
  190.0 2.3 copy.54
  192.3 2.5 %copy.55 = bf16[1,1024,512]{2,1,0:T(8,128)(2,1)} copy(bf16[1,1024,512]{1,2,0:T(8,128)(2,1)} %get-tuple-element.18) | data formatting | bytes 2097152
  194.8 37.3 %reduce-scatter.2.cloned.1.call-done = bf16[1024,512]{1,0:T(8,128)(2,1)} async-done(((bf16[1024,2048]{1,0:T(8,128)(2,1)}), bf16[1024,512]{1,0:T(8,128)(2,1)}) %reduce-scatter.2.cloned.1.call-update) | async-done | bytes 1048592 | tf_op jit(solution)/shard_map/reduce_scatter | solution.py:122
  232.1 2.6 %fusion.42 = bf16[1,1024,512]{2,1,0:T(8,128)(2,1)} fusion(bf16[1024,512]{1,0:T(8,128)(2,1)} %reduce-scatter.2.cloned.1.call-done, bf16[1,1024,512]{2,1,0:T(8,128)(2,1)S(1)} %copy-done.5, f32[512]{0:T(512)S(1)} %dynamic_slice.3, pred[1024]{0:T(1024)(128)(4,1)S(1)} %iota_compare_fusion.2), kind=kLoop, calls=%fused_computation.48 | loop fusion | flops 3145728 | bytes 3148800 | tf_op jit(solution)/shard_map/broadcast_in_dim | solution.py:128
  (50 shorter events, 0.2 us)
Async XLA Ops:
  7.2 176.4 %copy-start = (bf16[512,2048]{1,0:T(8,128)(2,1)S(1)}, bf16[512,2048]{1,0:T(8,128)(2,1)}, u32[]{:S(2)}) copy-start(bf16[512,2048]{1,0:T(8,128)(2,1)} %param.18) | copy-start | bytes 6291460
  7.2 39.6 %all-gather.10.cloned.1.call-start = ((), (), s32[]{:S(2)}) async-start(), calls=%async_computation.4 | async-start | bytes 5242880 | tf_op jit(solution)/shard_map/all_gather | solution.py:28
  7.9 92.0 %all-gather.6.cloned.1.call-start = ((), (), s32[]{:S(2)}) async-start(), calls=%async_computation.1 | async-start | bytes 2359296 | tf_op jit(solution)/shard_map/all_gather | solution.py:54
  9.8 141.5 %all-gather.8.cloned.1.call-start = ((), (), s32[]{:S(2)}) async-start(), calls=%async_computation.2 | async-start | bytes 2359296 | tf_op jit(solution)/shard_map/all_gather | solution.py:55
  11.6 220.5 %reduce-scatter.2.cloned.1.call-start = ((), (), s32[]{:S(2)}) async-start(), calls=%async_computation.3 | async-start | bytes 5242880 | tf_op jit(solution)/shard_map/reduce_scatter | solution.py:122
  40.2 13.0 %copy-start.15 = (f32[3,512]{1,0:T(4,128)S(1)}, f32[3,512]{1,0:T(4,128)}, u32[]{:S(2)}) copy-start(f32[3,512]{1,0:T(4,128)} %param.17) | copy-start | bytes 18436
  40.2 13.0 %copy-start.16 = (f32[2048]{0:T(1024)S(1)}, f32[2048]{0:T(1024)}, u32[]{:S(2)}) copy-start(f32[2048]{0:T(1024)} %param.15) | copy-start | bytes 24580
  40.2 13.0 %copy-start.17 = (f32[2048]{0:T(1024)S(1)}, f32[2048]{0:T(1024)}, u32[]{:S(2)}) copy-start(f32[2048]{0:T(1024)} %param.14) | copy-start | bytes 24580
  46.8 6.4 %copy-start.1 = (bf16[1,1024,2048]{2,1,0:T(8,128)(2,1)S(1)}, bf16[1,1024,2048]{2,1,0:T(8,128)(2,1)}, u32[]{:S(2)}) copy-start(bf16[1,1024,2048]{2,1,0:T(8,128)(2,1)} %all-gather.10.cloned.1.call-done) | copy-start | bytes 12582916
  64.5 35.4 %copy-start.14 = (f32[4]{0:T(128)S(1)}, f32[4]{0:T(128)}, u32[]{:S(2)}) copy-start(f32[4]{0:T(128)} %param.20) | copy-start | bytes 52
  117.8 4.6 %copy-start.3 = (f32[512,1024]{1,0:T(8,128)S(1)}, f32[512,1024]{1,0:T(8,128)}, u32[]{:S(2)}) copy-start(f32[512,1024]{1,0:T(8,128)} %get-tuple-element.34) | copy-start | bytes 6291460
  117.8 4.6 %copy-start.6 = (pred[512,1024]{1,0:T(8,128)(4,1)S(1)}, pred[512,1024]{1,0:T(8,128)(4,1)}, u32[]{:S(2)}) copy-start(pred[512,1024]{1,0:T(8,128)(4,1)} %get-tuple-element.27) | copy-start | bytes 1572868
  117.8 4.6 %copy-start.7 = (f32[512,1024]{1,0:T(8,128)S(1)}, f32[512,1024]{1,0:T(8,128)}, u32[]{:S(2)}) copy-start(f32[512,1024]{1,0:T(8,128)} %get-tuple-element.35) | copy-start | bytes 6291460
  117.8 4.6 %copy-start.10 = (bf16[1,1024,512]{1,2,0:T(8,128)(2,1)S(1)}, bf16[1,1024,512]{1,2,0:T(8,128)(2,1)}, u32[]{:S(2)}) copy-start(bf16[1,1024,512]{1,2,0:T(8,128)(2,1)} %get-tuple-element.21) | copy-start | bytes 3145732
  117.8 4.6 %copy-start.11 = (pred[512,1024]{1,0:T(8,128)(4,1)S(1)}, pred[512,1024]{1,0:T(8,128)(4,1)}, u32[]{:S(2)}) copy-start(pred[512,1024]{1,0:T(8,128)(4,1)} %get-tuple-element.28) | copy-start | bytes 1572868
  117.8 4.6 %copy-start.13 = (bf16[1,512,512]{1,2,0:T(8,128)(2,1)S(1)}, bf16[1,512,512]{1,2,0:T(8,128)(2,1)}, u32[]{:S(2)}) copy-start(bf16[1,512,512]{1,2,0:T(8,128)(2,1)} %get-tuple-element.24) | copy-start | bytes 1572868
  122.4 7.9 %copy-start.18 = (f32[4,512,1024]{2,1,0:T(8,128)}, f32[4,512,1024]{2,1,0:T(8,128)S(1)}, u32[]{:S(2)}) copy-start(f32[4,512,1024]{2,1,0:T(8,128)S(1)} %get-tuple-element.30) | copy-start | bytes 25165828
  151.3 15.1 %copy-start.4 = (f32[512,1024]{1,0:T(8,128)S(1)}, f32[512,1024]{1,0:T(8,128)}, u32[]{:S(2)}) copy-start(f32[512,1024]{1,0:T(8,128)} %get-tuple-element.34) | copy-start | bytes 6291460
  166.3 6.1 %copy-start.2 = (f32[4,512,1024]{2,1,0:T(8,128)S(1)}, f32[4,512,1024]{2,1,0:T(8,128)}, u32[]{:S(2)}) copy-start(f32[4,512,1024]{2,1,0:T(8,128)} %get-tuple-element.33) | copy-start | bytes 25165828
  166.4 6.1 %copy-start.9 = (bf16[1,1024,512]{1,2,0:T(8,128)(2,1)S(1)}, bf16[1,1024,512]{1,2,0:T(8,128)(2,1)}, u32[]{:S(2)}) copy-start(bf16[1,1024,512]{1,2,0:T(8,128)(2,1)} %get-tuple-element.20) | copy-start | bytes 3145732
  166.4 12.0 %slice-start = ((s8[8388608]{0:T(1024)(128)(4,1)}), s8[4194304]{0:T(1024)(128)(4,1)S(1)}, s32[]{:S(2)}) async-start(s8[8388608]{0:T(1024)(128)(4,1)} %bitcast.74), calls=%async_computation.5 | async-start | bytes 8388608
  172.4 5.9 %copy-start.8 = (f32[512,1024]{1,0:T(8,128)S(1)}, f32[512,1024]{1,0:T(8,128)}, u32[]{:S(2)}) copy-start(f32[512,1024]{1,0:T(8,128)} %get-tuple-element.35) | copy-start | bytes 6291460
  172.5 5.9 %copy-start.12 = (pred[512,1024]{1,0:T(8,128)(4,1)S(1)}, pred[512,1024]{1,0:T(8,128)(4,1)}, u32[]{:S(2)}) copy-start(pred[512,1024]{1,0:T(8,128)(4,1)} %get-tuple-element.28) | copy-start | bytes 1572868
  172.5 5.9 %slice-start.1 = ((s8[8388608]{0:T(1024)(128)(4,1)}), s8[4194304]{0:T(1024)(128)(4,1)S(1)}, s32[]{:S(2)}) async-start(s8[8388608]{0:T(1024)(128)(4,1)} %bitcast.74), calls=%async_computation.6 | async-start | bytes 8388608
  172.5 5.9 %copy-start.19 = (f32[4,1024,128]{2,1,0:T(8,128)S(1)}, f32[4,1024,128]{2,1,0:T(8,128)}, u32[]{:S(2)}) copy-start(f32[4,1024,128]{2,1,0:T(8,128)} %fusion.2) | copy-start | bytes 6291460
  183.5 48.6 %copy-start.5 = (bf16[1,1024,512]{2,1,0:T(8,128)(2,1)S(1)}, bf16[1,1024,512]{2,1,0:T(8,128)(2,1)}, u32[]{:S(2)}) copy-start(bf16[1,1024,512]{2,1,0:T(8,128)(2,1)} %param.13) | copy-start | bytes 3145732
Sparse Core Ops, SparseCore 0:
  9.6 37.1 all-gather.9
  48.8 51.0 all-gather.5
  102.0 49.2 all-gather.7
  189.3 42.6 reduce-scatter.1
where the time goes:
time: 242 us; the launch traced here: 241 us
  waiting for transfers between devices  79.7 us (33%)
  matrix products  71.7 us (30%)
  other arithmetic  39.6 us (16%)
  blocking collectives  22.2 us (9%)
  between operations  16.1 us (7%)
  local copies, waits for them, and re-layouts  11.6 us (5%)
    reduce_scatter x1, waiting for transfers between devices, on_device(): lax.psum_scatter(partial_value.astype(jnp.bfloat16), 'tp', scatter_dimens...  37.3 us
    all_gather x1, waiting for transfers between devices, on_device(): key_piece = lax.all_gather(prefix_k, 'req', axis=0, tiled=True)  32.2 us
    all_gather x1, blocking collectives, on_device(): number_piece = lax.all_gather(block_numbers, 'req', axis=0, tiled=True)  22.2 us
    dot_general x1, matrix products, on_device(): jnp.einsum('shd,khd->hsk', query_heads, compute_key_heads, preferred_elem...  17.8 us
    dot_general x1, matrix products, on_device(): jnp.einsum('hsk,khd->hsd', compute_weights.astype(jnp.bfloat16), compute_...  15.1 us
    reduce_sum x1, other arithmetic, on_device(): compute_new_sum = jnp.sum(compute_weights, axis=2)  14.3 us
    dot_general x2, matrix products, on_device(): jnp.einsum('shd,khd->hsk', query_block, key_heads, preferred_element_type...  12.3 us
    dot_general x1, matrix products, on_device(): jnp.einsum('sd,cdh->csh', normed, w_qkv, preferred_element_type=jnp.float32)  11.3 us
  transfers between devices with their start and end apart: 4, of which 4 were waited for; matrix products, arithmetic and copies ran while one was open for 34% of the time, Pallas kernels for 0%

commit v1 on v0

--- a/solution.py
+++ b/solution.py
@@ -5,6 +5,28 @@
 
 EPS = 1e-05
 NEGATIVE = -1e30
+
+
+def laid_out(parts, dim):
+    parts = jnp.moveaxis(parts, 0, dim)
+    shape = parts.shape
+    return parts.reshape(*shape[:dim], shape[dim] * shape[dim + 1], *shape[dim + 2 :])
+
+
+def ring_gather(array, axis, dim):
+    length = lax.axis_size(axis)
+    pairs = [(i, (i + 1) % length) for i in range(length)]
+    back = [(b, a) for a, b in pairs]
+    lower, upper = ([], [])
+    for hop in range(length - 1):
+        if hop % 2 == 0:
+            lower.append(lax.ppermute(lower[-1] if lower else array, axis, pairs))
+        else:
+            upper.append(lax.ppermute(upper[-1] if upper else array, axis, back))
+    tiles = jnp.stack([*lower[::-1], array, *upper])
+    shift = lax.axis_index(axis) - len(lower)
+    tiles = tiles[(jnp.arange(length) - shift) % length]
+    return laid_out(tiles, dim)
 
 
 def on_device(
@@ -51,7 +73,7 @@
     prefix_total = half_count * block_tokens
     block_numbers = jnp.full((block_tokens,), block_of_device[0], jnp.int32)
     query_pos = (prefix_total + slot_ids).astype(jnp.float32)
-    key_piece = lax.all_gather(prefix_k, "req", axis=0, tiled=True)
+    key_piece = ring_gather(prefix_k, "req", 0)
     value_piece = lax.all_gather(prefix_v, "req", axis=0, tiled=True)
     number_piece = lax.all_gather(block_numbers, "req", axis=0, tiled=True)
     count = key_piece.shape[0]

time: 242 us -> 246 us (1.017)
  waiting for transfers between devices: 79.7 us -> 60.5 us
  starting transfers between devices: 0.16 us -> 14 us
  local copies, waits for them, and re-layouts: 11.6 us -> 23 us
    all_gather x1 -> x0, waiting for transfers between devices: 32.2 us -> none  [on_device(): key_piece = lax.all_gather(prefix_k, 'req', axis=0, tiled=True)]
    ppermute x0 -> x7, waiting for transfers between devices: none -> 19.5 us  [the longest x4 12.1 us: ring_gather(): lower.append(lax.ppermute(lower[-1] if lower else array, axis, pairs))]
    ppermute x0 -> x7, starting transfers between devices: none -> 13.9 us  [the longest x3 7.83 us: ring_gather(): upper.append(lax.ppermute(upper[-1] if upper else array, axis, back))]
    all_gather x1, waiting for transfers between devices: 6.73 us -> 0.02 us  [on_device(): value_piece = lax.all_gather(prefix_v, 'req', axis=0, tiled=True)]
    another operation x0 -> x2, local copies, waits for them, and re-layouts: none -> 4.7 us  [the longest x1 3.98 us: on_device(): compute_key_heads = key_piece.reshape(count, heads_dev, head_size)]
    gather x0 -> x1, local copies, waits for them, and re-layouts: none -> 3.63 us  [ring_gather(): tiles = tiles[(jnp.arange(length) - shift) % length]]
    unnamed x49 -> x57, local copies, waits for them, and re-layouts: 8.48 us -> 11.5 us
    reduce_scatter x1, waiting for transfers between devices: 37.3 us -> 40.3 us  [on_device(): lax.psum_scatter(partial_value.astype(jnp.bfloat16), 'tp', scatter_dimens...]
  transfers between devices with their start and end apart: 4 -> 10, of which waited for: 4 -> 5; matrix products, arithmetic and copies ran while one was open for 34% -> 38% of each run, Pallas kernels for 0% -> 0%
where the time goes in v1:
time: 246 us
  matrix products  72.2 us (29%)
  waiting for transfers between devices  60.5 us (25%)
  other arithmetic  39.2 us (16%)
  local copies, waits for them, and re-layouts  23 us (9%)
  blocking collectives  20.7 us (8%)
  between operations  16.2 us (7%)
  starting transfers between devices  14 us (6%)
    reduce_scatter x1, waiting for transfers between devices, on_device(): lax.psum_scatter(partial_value.astype(jnp.bfloat16), 'tp', scatter_dimens...  40.3 us
    all_gather x1, blocking collectives, on_device(): number_piece = lax.all_gather(block_numbers, 'req', axis=0, tiled=True)  20.7 us
    dot_general x1, matrix products, on_device(): jnp.einsum('shd,khd->hsk', query_heads, compute_key_heads, preferred_elem...  18.4 us
    dot_general x1, matrix products, on_device(): jnp.einsum('hsk,khd->hsd', compute_weights.astype(jnp.bfloat16), compute_...  15.1 us
    reduce_sum x1, other arithmetic, on_device(): compute_new_sum = jnp.sum(compute_weights, axis=2)  14 us
    dot_general x2, matrix products, on_device(): jnp.einsum('shd,khd->hsk', query_block, key_heads, preferred_element_type...  12.5 us
    ppermute x4, waiting for transfers between devices, ring_gather(): lower.append(lax.ppermute(lower[-1] if lower else array, axis, pairs))  12.1 us
    unnamed x57, local copies, waits for them, and re-layouts  11.5 us
  transfers between devices with their start and end apart: 10, of which 5 were waited for; matrix products, arithmetic and copies ran while one was open for 38% of the time, Pallas kernels for 0%

profile of v1, /device:TPU:0, one launch (start us, length us, event | category | flops | bytes accessed | tf_op | source)
XLA Modules:
  0.0 245.8 jit_solution(11849957231965866649)
XLA Ops:
  7.2 0.7 all-gather.7.cloned.1.call-update
  7.9 0.0 all-gather.5.cloned.1.call-start
  8.0 3.0 %collective-permute-start = (bf16[256,512]{1,0:T(8,128)(2,1)}, bf16[256,512]{1,0:T(8,128)(2,1)S(1)}, u32[]{:S(2)}, u32[]{:S(2)}) collective-permute-start(bf16[256,512]{1,0:T(8,128)(2,1)} %param.21), channel_id=1, source_target_pairs={{0,4},{4,8},{8,12},{12,16},{16,20},{20,24},{24,28},{28,0},{1,5},{5... | collective-permute-start | bytes 786440 | tf_op jit(solution)/shard_map/ppermute | solution.py:23
  11.0 3.1 %collective-permute-start.4 = (bf16[256,512]{1,0:T(8,128)(2,1)}, bf16[256,512]{1,0:T(8,128)(2,1)S(1)}, u32[]{:S(2)}, u32[]{:S(2)}) collective-permute-start(bf16[256,512]{1,0:T(8,128)(2,1)} %param.21), channel_id=1, source_target_pairs={{4,0},{8,4},{12,8},{16,12},{20,16},{24,20},{28,24},{0,28},{5,1},{9... | collective-permute-start | bytes 786440 | tf_op jit(solution)/shard_map/ppermute | solution.py:25
  14.1 1.8 copy.44
  15.9 0.0 reduce-scatter.2.cloned.1.call-start
  16.6 20.7 %all-gather.1 = s32[8,1,256]{2,1,0:T(1,128)S(1)} all-gather(s32[1,1,256]{2,1,0:T(1,128)S(1)} %broadcast.232), channel_id=1, replica_groups=mesh['req'=8,'tp'=4] {'req'}, dimensions={0}, use_global_device_ids=true | all-gather | bytes 9216 | tf_op jit(solution)/shard_map/all_gather | solution.py:78
  37.3 3.8 %broadcast_subtract_fusion = f32[1024,2048]{1,0:T(8,128)} fusion(f32[2048]{0:T(1024)S(1)} %fusion.51, f32[1024]{0:T(1024)S(1)} %add_convert_fusion.1), kind=kLoop, calls=%fused_computation.29 | loop fusion | flops 2097152 | bytes 8400896 | tf_op jit(solution)/shard_map/sub | solution.py:93
  41.9 0.1 collective-permute-start.1
  42.0 2.3 subtract_convert_fusion
  44.3 6.8 %collective-permute-done.1 = bf16[256,512]{1,0:T(8,128)(2,1)S(1)} collective-permute-done((bf16[256,512]{1,0:T(8,128)(2,1)S(1)}, bf16[256,512]{1,0:T(8,128)(2,1)S(1)}, u32[]{:S(2)}, u32[]{:S(2)}) %collective-permute-start.1) | collective-permute-done | bytes 262176 | tf_op jit(solution)/shard_map/ppermute | solution.py:23
  51.1 1.7 fusion.36
  52.8 4.7 %collective-permute-start.5 = (bf16[256,512]{1,0:T(8,128)(2,1)S(1)}, bf16[256,512]{1,0:T(8,128)(2,1)S(1)}, u32[]{:S(2)}, u32[]{:S(2)}) collective-permute-start(bf16[256,512]{1,0:T(8,128)(2,1)S(1)} %collective-permute-done.4), channel_id=1, source_target_pairs={{4,0},{8,4},{12,8},{16,12},{20,16},{24,20},{28,24},{0,28},{5,1},{9... | collective-permute-start | bytes 786440 | tf_op jit(solution)/shard_map/ppermute | solution.py:25
  57.5 5.4 %collective-permute-done.2 = bf16[256,512]{1,0:T(8,128)(2,1)S(1)} collective-permute-done((bf16[256,512]{1,0:T(8,128)(2,1)S(1)}, bf16[256,512]{1,0:T(8,128)(2,1)S(1)}, u32[]{:S(2)}, u32[]{:S(2)}) %collective-permute-start.2) | collective-permute-done | bytes 262176 | tf_op jit(solution)/shard_map/ppermute | solution.py:23
  62.9 3.0 %collective-permute-start.3 = (bf16[256,512]{1,0:T(8,128)(2,1)S(1)}, bf16[256,512]{1,0:T(8,128)(2,1)S(1)}, u32[]{:S(2)}, u32[]{:S(2)}) collective-permute-start(bf16[256,512]{1,0:T(8,128)(2,1)S(1)} %collective-permute-done.2), channel_id=1, source_target_pairs={{0,4},{4,8},{8,12},{12,16},{16,20},{20,24},{24,28},{28,0},{1,5},{5... | collective-permute-start | bytes 786440 | tf_op jit(solution)/shard_map/ppermute | solution.py:23
  66.5 6.1 %collective-permute-done.5 = bf16[256,512]{1,0:T(8,128)(2,1)S(1)} collective-permute-done((bf16[256,512]{1,0:T(8,128)(2,1)S(1)}, bf16[256,512]{1,0:T(8,128)(2,1)S(1)}, u32[]{:S(2)}, u32[]{:S(2)}) %collective-permute-start.5) | collective-permute-done | bytes 262176 | tf_op jit(solution)/shard_map/ppermute | solution.py:25
  72.6 0.7 bitcast_dynamic-update-slice_fusion.7
  73.4 0.7 bitcast_dynamic-update-slice_fusion.6
  74.1 0.7 bitcast_dynamic-update-slice_fusion.5
  74.8 0.7 bitcast_dynamic-update-slice_fusion.4
  75.5 0.7 bitcast_dynamic-update-slice_fusion.3
  76.3 0.7 bitcast_dynamic-update-slice_fusion.2
  77.0 0.7 bitcast_dynamic-update-slice_fusion.1
  77.7 1.3 collective-permute-done.6
  79.0 0.7 bitcast_dynamic-update-slice_fusion
  79.7 3.6 %gather_fusion = bf16[8,256,512]{2,1,0:T(8,128)(2,1)} fusion(bf16[8,256,512]{2,1,0:T(8,128)(2,1)} %bitcast_dynamic-update-slice_fusion, s32[1024]{0:T(1024)S(1)} %pad_clamp_fusion), kind=kCustom, calls=%fused_computation | custom fusion | bytes 4194336 | tf_op jit(solution)/shard_map/gather | solution.py:28
  83.4 4.0 %reshape_reshape.3 = bf16[2048,4,128]{2,1,0:T(4,128)(2,1)} reshape(bf16[8,256,512]{2,1,0:T(8,128)(2,1)} %gather_fusion) | data formatting | bytes 4194304 | tf_op jit(solution)/shard_map/reshape;reshape | solution.py:84
  87.3 3.0 %convert_reduce_fusion = f32[1024]{0:T(1024)S(1)} fusion(bf16[1,1024,2048]{2,1,0:T(8,128)(2,1)} %all-gather.7.cloned.1.call-done), kind=kLoop, calls=%fused_computation.7 | loop fusion | flops 4193280 | bytes 4198400 | tf_op jit(solution)/shard_map/reduce_sum | solution.py:52
  90.3 3.4 %fusion.8 = f32[1024]{0:T(1024)S(1)} fusion(bf16[1,1024,2048]{2,1,0:T(8,128)(2,1)} %all-gather.7.cloned.1.call-done, f32[1024]{0:T(1024)S(1)} %broadcast_multiply_fusion), kind=kLoop, calls=%fused_computation.12 | loop fusion | flops 8387584 | bytes 4202496 | tf_op jit(solution)/shard_map/reduce_sum | solution.py:53
  93.8 11.1 %fusion.29 = bf16[3,1024,512]{1,2,0:T(8,128)(2,1)S(1)} fusion(f32[3,512]{1,0:T(4,128)S(1)} %copy-done.16, bf16[3,2048,512]{2,1,0:T(8,128)(2,1)} %param.16, bf16[1,1024,2048]{2,1,0:T(8,128)(2,1)S(1)} %copy-done.1, f32[2048]{0:T(1024)S(1)} %copy-done.17, f32[2048]{0:T(1024)S(1)} %copy-done.18, f32[1024]{0:T(1024)S(1)} %add_sqrt_fusion, ...), kind=kOutput, calls=%fused_computation.37 | convolution fusion | flops 6458179584 | bytes 13662208 | tf_op jit(solution)/shard_map/sd,cdh->csh/dot_general | solution.py:56
  104.9 2.1 broadcast_select_fusion
  107.0 1.0 fusion.68
  108.1 18.4 %fusion.69 = (f32[4,1024]{1,0:T(4,128)S(1)}, f32[4,1024,2048]{2,1,0:T(8,128)}) fusion(f32[1024,2048]{1,0:T(8,128)} %broadcast_subtract_fusion, f32[4]{0:T(128)S(1)} %copy-done.15, bf16[1024,4,128]{0,2,1:T(8,128)(2,1)S(1)} %bitcast.78, bf16[2048,4,128]{2,1,0:T(4,128)(2,1)} %reshape_reshape.3, pred[2048]{0:T(1024)(128)(4,1)S(1)} %fusion.48), kind=kOutput, calls=%fused_computation.111 | convolution fusion | flops 2189422592 | bytes 45107216 | tf_op jit(solution)/shard_map/shd,khd->hsk/dot_general | solution.py:87
  126.5 4.7 %fusion.16 = (f32[4,512]{1,0:T(4,128)S(1)}, f32[4,512,1024]{2,1,0:T(8,128)S(1)}) fusion(f32[512,1024]{1,0:T(8,128)} %get-tuple-element.35, f32[4]{0:T(128)S(1)} %copy-done.15, pred[512,1024]{1,0:T(8,128)(4,1)} %get-tuple-element.28, bf16[512,4,128]{0,2,1:T(8,128)(2,1)} %bitcast.85, bf16[1024,4,128]{0,2,1:T(8,128)(2,1)} %bitcast.81), kind=kOutput, calls=%fused_computation.25 | convolution fusion | flops 547354624 | bytes 12591120 | tf_op jit(solution)/shard_map/shd,khd->hsk/dot_general | solution.py:116
  131.3 7.8 %fusion.12 = (f32[4,512]{1,0:T(4,128)S(1)}, f32[4,512]{1,0:T(4,128)S(1)}, f32[4,512,1024]{2,1,0:T(8,128)}) fusion(f32[4,512,1024]{2,1,0:T(8,128)S(1)} %get-tuple-element.30, f32[4,512]{1,0:T(4,128)S(1)} %slice_maximum_fusion.1, f32[512,1024]{1,0:T(8,128)S(1)} %copy-done.7, f32[4]{0:T(128)S(1)} %copy-done.15, pred[512,1024]{1,0:T(8,128)(4,1)S(1)} %copy-done.11, ...), kind=kOutput, calls=%fused_computation.20 | convolution fusion | flops 562032640 | bytes 23617552 | tf_op jit(solution)/shard_map/shd,khd->hsk/dot_general | solution.py:116
  139.1 14.0 %fusion = f32[4,1024]{1,0:T(4,128)S(1)} fusion(f32[4,1024,2048]{2,1,0:T(8,128)} %get-tuple-element.32, f32[4,1024]{1,0:T(4,128)S(1)} %broadcast_maximum_fusion, pred[2048]{0:T(1024)(128)(4,1)S(1)} %fusion.48), kind=kLoop, calls=%fused_computation.3 | loop fusion | flops 25161728 | bytes 33589248 | tf_op jit(solution)/shard_map/reduce_sum | solution.py:100
  153.2 15.1 %fusion.2 = f32[4,1024,128]{2,1,0:T(8,128)} fusion(bf16[2048,4,128]{0,2,1:T(8,128)(2,1)} %bitcast.88, f32[4,1024,2048]{2,1,0:T(8,128)} %get-tuple-element.32, f32[4,1024]{1,0:T(4,128)S(1)} %broadcast_maximum_fusion, pred[2048]{0:T(1024)(128)(4,1)S(1)} %fusion.48), kind=kOutput, calls=%fused_computation.5 | convolution fusion | flops 2172649472 | bytes 37767168 | tf_op jit(solution)/shard_map/hsk,khd->hsd/dot_general | solution.py:101
  168.3 6.0 %fusion.14 = f32[4,512]{1,0:T(4,128)S(1)} fusion(f32[4,512,1024]{2,1,0:T(8,128)} %get-tuple-element.33, f32[4,512]{1,0:T(4,128)S(1)} %slice_maximum_fusion, f32[512,1024]{1,0:T(8,128)S(1)} %copy-done.4, f32[4]{0:T(128)S(1)} %copy-done.15, pred[512,1024]{1,0:T(8,128)(4,1)S(1)} %copy-done.6), kind=kLoop, calls=%fused_computation.22 | loop fusion | flops 14678016 | bytes 11026448 | tf_op jit(solution)/shard_map/reduce_sum | solution.py:130
  174.4 5.8 %divide_convert_fusion = bf16[4,512,128]{2,1,0:T(8,128)(2,1)S(1)} fusion(bf16[1024,4,128]{0,2,1:T(8,128)(2,1)S(1)} %bitcast.79, f32[4,512,1024]{2,1,0:T(8,128)S(1)} %copy-done.2, f32[4,512]{1,0:T(4,128)S(1)} %slice_maximum_fusion, f32[512,1024]{1,0:T(8,128)S(1)} %copy-done.4, f32[4]{0:T(128)S(1)} %copy-done.15, pred[512,1024]{1,0:T(8,128)(4,1)S(1)} %copy-done.6, ...), kind=kOutput, calls=%fused_computation.54 | convolution fusion | flops 552599552 | bytes 13656080 | tf_op jit(solution)/shard_map/hsk,khd->hsd/dot_general | solution.py:131
  180.3 3.8 %divide_convert_fusion.1 = bf16[4,512,128]{2,1,0:T(8,128)(2,1)S(1)} fusion(bf16[1024,4,128]{0,2,1:T(8,128)(2,1)S(1)} %bitcast.80, f32[4,512,1024]{2,1,0:T(8,128)S(1)} %bitcast.90, f32[4,512]{1,0:T(4,128)S(1)} %slice_maximum_fusion.1, f32[512,1024]{1,0:T(8,128)S(1)} %copy-done.8, f32[4]{0:T(128)S(1)} %copy-done.15, pred[512,1024]{1,0:T(8,128)(4,1)S(1)} %copy-done.12, ...), kind=kOutput, calls=%fused_computation.55 | convolution fusion | flops 552599552 | bytes 13656080 | tf_op jit(solution)/shard_map/hsk,khd->hsd/dot_general | solution.py:131
  184.0 0.1 maximum_bitcast_fusion
  184.1 1.3 copy.52
  185.4 5.6 %convolution_convert_fusion = bf16[1024,2048]{1,0:T(8,128)(2,1)} fusion(bf16[1024,512]{0,1:T(8,128)(2,1)} %bitcast.83, bf16[512,2048]{1,0:T(8,128)(2,1)S(1)} %copy-done), kind=kOutput, calls=%fused_computation.36 | convolution fusion | flops 2149580800 | bytes 7340032 | tf_op jit(solution)/shard_map/dot_general | solution.py:143
  191.1 0.8 dynamic_slice.3
  191.9 2.3 copy.53
  194.1 2.3 copy.54
  196.4 40.3 %reduce-scatter.2.cloned.1.call-done = bf16[1024,512]{1,0:T(8,128)(2,1)} async-done(((bf16[1024,2048]{1,0:T(8,128)(2,1)}), bf16[1024,512]{1,0:T(8,128)(2,1)}) %reduce-scatter.2.cloned.1.call-update) | async-done | bytes 1048592 | tf_op jit(solution)/shard_map/reduce_scatter | solution.py:144
  236.7 2.6 %fusion.43 = bf16[1,1024,512]{2,1,0:T(8,128)(2,1)} fusion(bf16[1024,512]{1,0:T(8,128)(2,1)} %reduce-scatter.2.cloned.1.call-done, bf16[1,1024,512]{2,1,0:T(8,128)(2,1)S(1)} %copy-done.5, f32[512]{0:T(512)S(1)} %dynamic_slice.3, pred[1024]{0:T(1024)(128)(4,1)S(1)} %iota_compare_fusion.2), kind=kLoop, calls=%fused_computation.50 | loop fusion | flops 3145728 | bytes 3148800 | tf_op jit(solution)/shard_map/broadcast_in_dim | solution.py:150
  (74 shorter events, 0.3 us)
Async XLA Ops:
  7.2 178.3 %copy-start = (bf16[512,2048]{1,0:T(8,128)(2,1)S(1)}, bf16[512,2048]{1,0:T(8,128)(2,1)}, u32[]{:S(2)}) copy-start(bf16[512,2048]{1,0:T(8,128)(2,1)} %param.18) | copy-start | bytes 6291460
  7.2 80.2 %all-gather.7.cloned.1.call-start = ((), (), s32[]{:S(2)}) async-start(), calls=%async_computation.3 | async-start | bytes 5242880 | tf_op jit(solution)/shard_map/all_gather | solution.py:50
  7.9 67.6 %copy-start.14 = (bf16[256,512]{1,0:T(8,128)(2,1)S(1)}, bf16[256,512]{1,0:T(8,128)(2,1)}, u32[]{:S(2)}) copy-start(bf16[256,512]{1,0:T(8,128)(2,1)} %param.21) | copy-start | bytes 786436
  7.9 145.2 %all-gather.5.cloned.1.call-start = ((), (), s32[]{:S(2)}) async-start(), calls=%async_computation.1 | async-start | bytes 2359296 | tf_op jit(solution)/shard_map/all_gather | solution.py:77
  8.0 33.9 %collective-permute-start = (bf16[256,512]{1,0:T(8,128)(2,1)}, bf16[256,512]{1,0:T(8,128)(2,1)S(1)}, u32[]{:S(2)}, u32[]{:S(2)}) collective-permute-start(bf16[256,512]{1,0:T(8,128)(2,1)} %param.21), channel_id=1, source_target_pairs={{0,4},{4,8},{8,12},{12,16},{16,20},{20,24},{24,28},{28,0},{1,5},{5... | collective-permute-start | bytes 786440 | tf_op jit(solution)/shard_map/ppermute | solution.py:23
  11.0 41.8 %collective-permute-start.4 = (bf16[256,512]{1,0:T(8,128)(2,1)}, bf16[256,512]{1,0:T(8,128)(2,1)S(1)}, u32[]{:S(2)}, u32[]{:S(2)}) collective-permute-start(bf16[256,512]{1,0:T(8,128)(2,1)} %param.21), channel_id=1, source_target_pairs={{4,0},{8,4},{12,8},{16,12},{20,16},{24,20},{28,24},{0,28},{5,1},{9... | collective-permute-start | bytes 786440 | tf_op jit(solution)/shard_map/ppermute | solution.py:25
  15.9 220.8 %reduce-scatter.2.cloned.1.call-start = ((), (), s32[]{:S(2)}) async-start(), calls=%async_computation.2 | async-start | bytes 5242880 | tf_op jit(solution)/shard_map/reduce_scatter | solution.py:144
  41.9 9.2 %collective-permute-start.1 = (bf16[256,512]{1,0:T(8,128)(2,1)S(1)}, bf16[256,512]{1,0:T(8,128)(2,1)S(1)}, u32[]{:S(2)}, u32[]{:S(2)}) collective-permute-start(bf16[256,512]{1,0:T(8,128)(2,1)S(1)} %collective-permute-done), channel_id=1, source_target_pairs={{0,4},{4,8},{8,12},{12,16},{16,20},{20,24},{24,28},{28,0},{1,5},{5... | collective-permute-start | bytes 786440 | tf_op jit(solution)/shard_map/ppermute | solution.py:23
  51.1 11.8 %collective-permute-start.2 = (bf16[256,512]{1,0:T(8,128)(2,1)S(1)}, bf16[256,512]{1,0:T(8,128)(2,1)S(1)}, u32[]{:S(2)}, u32[]{:S(2)}) collective-permute-start(bf16[256,512]{1,0:T(8,128)(2,1)S(1)} %collective-permute-done.1), channel_id=1, source_target_pairs={{0,4},{4,8},{8,12},{12,16},{16,20},{20,24},{24,28},{28,0},{1,5},{5... | collective-permute-start | bytes 786440 | tf_op jit(solution)/shard_map/ppermute | solution.py:23
  52.8 19.8 %collective-permute-start.5 = (bf16[256,512]{1,0:T(8,128)(2,1)S(1)}, bf16[256,512]{1,0:T(8,128)(2,1)S(1)}, u32[]{:S(2)}, u32[]{:S(2)}) collective-permute-start(bf16[256,512]{1,0:T(8,128)(2,1)S(1)} %collective-permute-done.4), channel_id=1, source_target_pairs={{4,0},{8,4},{12,8},{16,12},{20,16},{24,20},{28,24},{0,28},{5,1},{9... | collective-permute-start | bytes 786440 | tf_op jit(solution)/shard_map/ppermute | solution.py:25
  62.9 9.8 %collective-permute-start.3 = (bf16[256,512]{1,0:T(8,128)(2,1)S(1)}, bf16[256,512]{1,0:T(8,128)(2,1)S(1)}, u32[]{:S(2)}, u32[]{:S(2)}) collective-permute-start(bf16[256,512]{1,0:T(8,128)(2,1)S(1)} %collective-permute-done.2), channel_id=1, source_target_pairs={{0,4},{4,8},{8,12},{12,16},{16,20},{20,24},{24,28},{28,0},{1,5},{5... | collective-permute-start | bytes 786440 | tf_op jit(solution)/shard_map/ppermute | solution.py:23
  72.6 6.4 %collective-permute-start.6 = (bf16[256,512]{1,0:T(8,128)(2,1)S(1)}, bf16[256,512]{1,0:T(8,128)(2,1)S(1)}, u32[]{:S(2)}, u32[]{:S(2)}) collective-permute-start(bf16[256,512]{1,0:T(8,128)(2,1)S(1)} %collective-permute-done.5), channel_id=1, source_target_pairs={{4,0},{8,4},{12,8},{16,12},{20,16},{24,20},{28,24},{0,28},{5,1},{9... | collective-permute-start | bytes 786440 | tf_op jit(solution)/shard_map/ppermute | solution.py:25
  79.7 14.0 %copy-start.16 = (f32[3,512]{1,0:T(4,128)S(1)}, f32[3,512]{1,0:T(4,128)}, u32[]{:S(2)}) copy-start(f32[3,512]{1,0:T(4,128)} %param.17) | copy-start | bytes 18436
  79.7 14.0 %copy-start.17 = (f32[2048]{0:T(1024)S(1)}, f32[2048]{0:T(1024)}, u32[]{:S(2)}) copy-start(f32[2048]{0:T(1024)} %param.15) | copy-start | bytes 24580
  79.7 14.0 %copy-start.18 = (f32[2048]{0:T(1024)S(1)}, f32[2048]{0:T(1024)}, u32[]{:S(2)}) copy-start(f32[2048]{0:T(1024)} %param.14) | copy-start | bytes 24580
  87.3 6.4 %copy-start.1 = (bf16[1,1024,2048]{2,1,0:T(8,128)(2,1)S(1)}, bf16[1,1024,2048]{2,1,0:T(8,128)(2,1)}, u32[]{:S(2)}) copy-start(bf16[1,1024,2048]{2,1,0:T(8,128)(2,1)} %all-gather.7.cloned.1.call-done) | copy-start | bytes 12582916
  104.9 3.2 %copy-start.15 = (f32[4]{0:T(128)S(1)}, f32[4]{0:T(128)}, u32[]{:S(2)}) copy-start(f32[4]{0:T(128)} %param.20) | copy-start | bytes 52
  126.4 4.8 %copy-start.3 = (f32[512,1024]{1,0:T(8,128)S(1)}, f32[512,1024]{1,0:T(8,128)}, u32[]{:S(2)}) copy-start(f32[512,1024]{1,0:T(8,128)} %get-tuple-element.34) | copy-start | bytes 6291460
  126.4 4.8 %copy-start.6 = (pred[512,1024]{1,0:T(8,128)(4,1)S(1)}, pred[512,1024]{1,0:T(8,128)(4,1)}, u32[]{:S(2)}) copy-start(pred[512,1024]{1,0:T(8,128)(4,1)} %get-tuple-element.27) | copy-start | bytes 1572868
  126.4 4.8 %copy-start.7 = (f32[512,1024]{1,0:T(8,128)S(1)}, f32[512,1024]{1,0:T(8,128)}, u32[]{:S(2)}) copy-start(f32[512,1024]{1,0:T(8,128)} %get-tuple-element.35) | copy-start | bytes 6291460
  126.5 4.8 %copy-start.10 = (bf16[1,1024,512]{1,2,0:T(8,128)(2,1)S(1)}, bf16[1,1024,512]{1,2,0:T(8,128)(2,1)}, u32[]{:S(2)}) copy-start(bf16[1,1024,512]{1,2,0:T(8,128)(2,1)} %get-tuple-element.21) | copy-start | bytes 3145732
  126.5 4.8 %copy-start.11 = (pred[512,1024]{1,0:T(8,128)(4,1)S(1)}, pred[512,1024]{1,0:T(8,128)(4,1)}, u32[]{:S(2)}) copy-start(pred[512,1024]{1,0:T(8,128)(4,1)} %get-tuple-element.28) | copy-start | bytes 1572868
  126.5 4.8 %copy-start.13 = (bf16[1,512,512]{1,2,0:T(8,128)(2,1)S(1)}, bf16[1,512,512]{1,2,0:T(8,128)(2,1)}, u32[]{:S(2)}) copy-start(bf16[1,512,512]{1,2,0:T(8,128)(2,1)} %get-tuple-element.24) | copy-start | bytes 1572868
  131.2 7.9 %copy-start.19 = (f32[4,512,1024]{2,1,0:T(8,128)}, f32[4,512,1024]{2,1,0:T(8,128)S(1)}, u32[]{:S(2)}) copy-start(f32[4,512,1024]{2,1,0:T(8,128)S(1)} %get-tuple-element.30) | copy-start | bytes 25165828
  153.2 15.1 %copy-start.4 = (f32[512,1024]{1,0:T(8,128)S(1)}, f32[512,1024]{1,0:T(8,128)}, u32[]{:S(2)}) copy-start(f32[512,1024]{1,0:T(8,128)} %get-tuple-element.34) | copy-start | bytes 6291460
  168.2 6.1 %copy-start.2 = (f32[4,512,1024]{2,1,0:T(8,128)S(1)}, f32[4,512,1024]{2,1,0:T(8,128)}, u32[]{:S(2)}) copy-start(f32[4,512,1024]{2,1,0:T(8,128)} %get-tuple-element.33) | copy-start | bytes 25165828
  168.2 6.1 %copy-start.9 = (bf16[1,1024,512]{1,2,0:T(8,128)(2,1)S(1)}, bf16[1,1024,512]{1,2,0:T(8,128)(2,1)}, u32[]{:S(2)}) copy-start(bf16[1,1024,512]{1,2,0:T(8,128)(2,1)} %get-tuple-element.20) | copy-start | bytes 3145732
  168.2 12.0 %slice-start = ((s8[8388608]{0:T(1024)(128)(4,1)}), s8[4194304]{0:T(1024)(128)(4,1)S(1)}, s32[]{:S(2)}) async-start(s8[8388608]{0:T(1024)(128)(4,1)} %bitcast.89), calls=%async_computation.4 | async-start | bytes 8388608
  174.3 5.9 %copy-start.8 = (f32[512,1024]{1,0:T(8,128)S(1)}, f32[512,1024]{1,0:T(8,128)}, u32[]{:S(2)}) copy-start(f32[512,1024]{1,0:T(8,128)} %get-tuple-element.35) | copy-start | bytes 6291460
  174.3 5.9 %copy-start.12 = (pred[512,1024]{1,0:T(8,128)(4,1)S(1)}, pred[512,1024]{1,0:T(8,128)(4,1)}, u32[]{:S(2)}) copy-start(pred[512,1024]{1,0:T(8,128)(4,1)} %get-tuple-element.28) | copy-start | bytes 1572868
  174.3 5.9 %slice-start.1 = ((s8[8388608]{0:T(1024)(128)(4,1)}), s8[4194304]{0:T(1024)(128)(4,1)S(1)}, s32[]{:S(2)}) async-start(s8[8388608]{0:T(1024)(128)(4,1)} %bitcast.89), calls=%async_computation.5 | async-start | bytes 8388608
  174.4 5.9 %copy-start.20 = (f32[4,1024,128]{2,1,0:T(8,128)S(1)}, f32[4,1024,128]{2,1,0:T(8,128)}, u32[]{:S(2)}) copy-start(f32[4,1024,128]{2,1,0:T(8,128)} %fusion.2) | copy-start | bytes 6291460
  185.4 51.3 %copy-start.5 = (bf16[1,1024,512]{2,1,0:T(8,128)(2,1)S(1)}, bf16[1,1024,512]{2,1,0:T(8,128)(2,1)}, u32[]{:S(2)}) copy-start(bf16[1,1024,512]{2,1,0:T(8,128)(2,1)} %param.13) | copy-start | bytes 3145732
Sparse Core Ops, SparseCore 0:
  9.6 37.1 all-gather.6
  48.8 59.1 all-gather.4
  191.2 45.4 reduce-scatter.1
